TPU v7x, 128 devices: a whole 4x4x4 slice. The times are simulated.
128 devices in a mesh: group: 4 (over y_hi, core), member: 32 (over x, y_lo, z).
Axes of the slice: x: 4, y: 4 (y_hi: 2, y_lo: 2; y = y_hi * 2 + y_lo), z: 4, core: 2. Of those that a mesh axis runs over, the one named last changes fastest.
Arguments:
- face_schur: float32 [512, 6, 256, 256], P(('group', 'member')), as said below
- face_inverse: float32 [512, 6, 256, 256], P(('group', 'member')), as said below
- face_basis: float32 [512, 6, 96, 256], P(('group', 'member')), may hold values from -6 to 6
- partner: int32 [512, 6], P(('group', 'member')), may hold values from 0 to 3071, as said below
- prim_index: int32 [512, 96], P(('group', 'member')), may hold values from 0 to 24575
Outputs:
- deluxe_basis: float32 [512, 6, 96, 256], P(('group', 'member'))
- coarse_blocks: float32 [512, 9216], P('group')
Inputs may be any that keep to these rules, and one draw needn't show every extreme that they name: partner pairs the faces: the partner of the partner of a face is the face itself; a face of subdomain s has its partner on another device of the same group, where subdomain s lies on device s // 4 and devices k * 32 to (k + 1) * 32 - 1 form group k; at most 1 faces of one device have partners on one other device, and some pair of devices has exactly 1. Every block of face_schur is exactly symmetric and positive definite. Every block of face_inverse is exactly symmetric.
All inputs are finite; a program needn't handle non-finite values.
Results may differ from a plain program's by a relative error of at most 0.0003.
Values sent between devices are 32-bit elements; how exact they have to be, the bound alone decides.
No kernel may reach another device: no remote copies, remote signals or barrier semaphores. Data moves between devices by JAX's collectives and lax.ppermute only.
A program may use at most 128 MiB of HBM per device.

v0:
```python
import jax
import jax.numpy as jnp
from jax import lax
from jax.sharding import PartitionSpec as P

SWEEPS = 2
COARSE_PER_SUB = 48
FULL_PRECISION = lax.Precision.HIGHEST


def inverse_sweeps(summed, initial):
    doubled = 2.0 * jnp.eye(summed.shape[-1], dtype=jnp.float32)
    current = initial
    for repeat in range(SWEEPS):
        applied = jnp.einsum("fij,fjk->fik", summed, current, precision=FULL_PRECISION)
        current = jnp.einsum("fij,fjk->fik", current, doubled - applied, precision=FULL_PRECISION)
    return current


def face_terms(own_schur, other_schur, own_inverse, other_inverse, basis):
    summed = own_schur + other_schur
    approx_inverse = inverse_sweeps(summed, 0.25 * (own_inverse + other_inverse))
    product = jnp.einsum("fck,fjk->fcj", basis, own_schur, precision=FULL_PRECISION)
    deluxe = jnp.einsum("fck,fik->fci", product, approx_inverse, precision=FULL_PRECISION)
    weighted = jnp.einsum("fci,fij->fcj", deluxe, other_schur, precision=FULL_PRECISION)
    face_block = jnp.einsum("fcj,fdj->fcd", weighted, deluxe, precision=FULL_PRECISION)
    return (deluxe, face_block)


def assemble_diagonal(local_diagonal):
    return lax.psum(local_diagonal, ("group", "member"))


def local(face_schur, face_inverse, face_basis, partner, prim_index):
    sub_count = face_schur.shape[0]
    face_width = face_schur.shape[-1]
    prim_count = face_basis.shape[2]
    face_count = sub_count * 6
    members = lax.axis_size("member")
    groups = lax.axis_size("group")
    capacity = (face_count + members - 2) // (members - 1)
    own_schur = face_schur.reshape(face_count, face_width, face_width)
    own_inverse = face_inverse.reshape(face_count, face_width, face_width)
    basis = face_basis.reshape(face_count, prim_count, face_width)
    targets = partner.reshape(face_count)
    target_member = targets // face_count % members
    target_local = targets % face_count
    same_peer = target_member[:, None] == target_member[None, :]
    order_index = jnp.arange(face_count, dtype=jnp.int32)
    send_rank = jnp.sum(same_peer & (order_index[None, :] < order_index[:, None]), axis=1)
    recv_rank = jnp.sum(same_peer & (target_local[None, :] < target_local[:, None]), axis=1)
    stacked = jnp.stack([own_schur, own_inverse], axis=1)
    buffer = (
        jnp.zeros((members, capacity) + stacked.shape[1:], jnp.float32)
        .at[target_member, send_rank]
        .set(stacked)
    )
    received = lax.all_to_all(buffer, "member", split_axis=0, concat_axis=0, tiled=True)
    picked = received[target_member, recv_rank]
    deluxe, face_block = face_terms(own_schur, picked[:, 0], own_inverse, picked[:, 1], basis)
    galerkin = jnp.sum(face_block.reshape(sub_count, 6, prim_count, prim_count), axis=1)
    diagonal_terms = jnp.diagonal(galerkin, axis1=1, axis2=2)
    coarse_total = COARSE_PER_SUB * sub_count * groups * members
    local_diagonal = (
        jnp.zeros((coarse_total,), jnp.float32)
        .at[prim_index.reshape(-1)]
        .add(diagonal_terms.reshape(-1))
    )
    assembled = assemble_diagonal(local_diagonal)
    scales = 1.0 / jnp.sqrt(assembled[prim_index])
    scaled = scales[:, :, None] * galerkin * scales[:, None, :]
    coarse_blocks = lax.all_gather(
        scaled.reshape(sub_count, prim_count * prim_count), "member", axis=0, tiled=True
    )
    deluxe_basis = deluxe.reshape(sub_count, 6, prim_count, face_width)
    return (deluxe_basis, coarse_blocks)


def solution(mesh):
    in_specs = (
        P(("group", "member"), None, None, None),
        P(("group", "member"), None, None, None),
        P(("group", "member"), None, None, None),
        P(("group", "member"), None),
        P(("group", "member"), None),
    )
    out_specs = (P(("group", "member"), None, None, None), P("group", None))
    return jax.shard_map(local, mesh=mesh, in_specs=in_specs, out_specs=out_specs, check_vma=False)
```

profile of v0, /device:TPU:0, one launch (start us, length us, event | category | flops | bytes accessed | tf_op | source)
XLA Modules:
  0.0 763.6 jit_solution(1772734053315307162)
XLA Ops:
  7.2 0.0 copy-start
  7.2 0.8 broadcast_divide_fusion
  8.0 0.7 compare_and_fusion.2
  8.7 0.1 div.30
  8.8 0.1 div.29
  8.9 0.1 rem.85
  9.0 0.1 ne.108
  9.1 0.1 and.74
  9.2 0.2 convert_reduce_fusion
  9.4 10.6 %pad_maximum_fusion = f32[24,2,256,256]{3,2,1,0:T(8,128)} fusion(f32[24,1,256,256]{3,2,1,0:T(8,128)} %bitcast.62, f32[24,1,256,256]{3,2,1,0:T(8,128)} %bitcast.58), kind=kLoop, calls=%fused_computation.5 | loop fusion | flops 3145728 | bytes 25165824 | tf_op jit(solution)/shard_map/stack | solution.py:52
  20.0 7.8 %broadcast.301 = f32[32,2,256,256]{3,2,1,0:T(8,128)} broadcast(f32[]{:T(128)} %constant.47.clone.1), dimensions={} | broadcast | bytes 16777220 | tf_op jit(solution)/shard_map/broadcast_in_dim | solution.py:54
  27.7 23.2 %scatter_fusion = f32[32,2,256,256]{3,2,1,0:T(8,128)} fusion(f32[32,2,256,256]{3,2,1,0:T(8,128)} %broadcast.301, s32[24]{0:T(128)S(1)} %fusion.24, f32[24,2,256,256]{3,2,1,0:T(8,128)} %pad_maximum_fusion), kind=kCustom, calls=%fused_computation.3 | custom fusion | bytes 37748832 | tf_op jit(solution)/shard_map/scatter | solution.py:56
  50.9 0.0 copy-start.6
  50.9 9.3 %all-to-all-start = ((f32[32,1,2,256,256]{4,3,2,1,0:T(8,128)}), f32[32,1,2,256,256]{4,3,2,1,0:T(8,128)}, u32[]{:S(2)}, u32[]{:S(2)}) async-start(f32[32,1,2,256,256]{4,3,2,1,0:T(8,128)} %bitcast.57), calls=%async_computation | async-start | bytes 33554432 | tf_op jit(solution)/shard_map/all_to_all | solution.py:58
  60.2 0.0 all-reduce.2.cloned.1.call-start
  60.2 0.0 copy-done.6
  60.2 0.1 reshape.256
  60.3 0.1 reshape.273
  60.5 0.0 copy-done
  60.5 10.1 %fusion.25 = f32[24,96,256]{2,1,0:T(8,128)} fusion(f32[24,96,256]{2,1,0:T(8,128)S(1)} %bitcast.56, f32[24,256,256]{2,1,0:T(8,128)} %bitcast.59), kind=kOutput, calls=%fused_computation.59 | convolution fusion | flops 1811939328 | bytes 11010048 | tf_op jit(solution)/shard_map/fck,fjk->fcj/dot_general | solution.py:23
  70.6 262.5 %all-to-all-done = f32[32,1,2,256,256]{4,3,2,1,0:T(8,128)} async-done(((f32[32,1,2,256,256]{4,3,2,1,0:T(8,128)}), f32[32,1,2,256,256]{4,3,2,1,0:T(8,128)}, u32[]{:S(2)}, u32[]{:S(2)}) %all-to-all-start) | async-done | bytes 16777248 | tf_op jit(solution)/shard_map/all_to_all | solution.py:58
  333.0 13.5 %gather_fusion = f32[24,2,256,256]{3,2,1,0:T(8,128)} fusion(f32[32,1,2,256,256]{4,3,2,1,0:T(8,128)} %all-to-all-done, s32[24]{0:T(128)S(1)} %get-tuple-element.4), kind=kCustom, calls=%fused_computation | custom fusion | bytes 25166016 | tf_op jit(solution)/shard_map/gather | solution.py:59
  346.5 0.0 copy-start.2
  346.5 9.0 %fusion.1 = f32[24,256,256]{2,1,0:T(8,128)} fusion(f32[24,2,256,256]{3,2,1,0:T(8,128)} %gather_fusion, f32[4,6,256,256]{3,2,1,0:T(8,128)} %param.6), kind=kLoop, calls=%fused_computation.9 | loop fusion | flops 3145728 | bytes 18874368 | tf_op jit(solution)/shard_map/mul | solution.py:22
  355.5 1.4 copy-done.2
  357.0 13.8 %fusion.12 = f32[24,256,256]{2,1,0:T(8,128)} fusion(f32[24,256,256]{2,1,0:T(8,128)} %fusion.1, f32[24,256,256]{2,1,0:T(8,128)} %bitcast.60, f32[24,2,256,256]{3,2,1,0:T(8,128)S(1)} %copy-done.2), kind=kOutput, calls=%fused_computation.19 | convolution fusion | flops 4833411072 | bytes 25165824 | tf_op jit(solution)/shard_map/fij,fjk->fik/dot_general | solution.py:15
  370.7 14.0 %fusion.4 = f32[24,256,256]{2,1,0:T(8,128)} fusion(f32[24,256,256]{2,1,0:T(8,128)} %fusion.1, f32[24,256,256]{2,1,0:T(8,128)} %fusion.12, f32[256,256]{1,0:T(8,128)S(1)} %fusion.14), kind=kOutput, calls=%fused_computation.12 | convolution fusion | flops 4833411072 | bytes 19136512 | tf_op jit(solution)/shard_map/fij,fjk->fik/dot_general | solution.py:16
  384.8 14.0 %fusion.10 = f32[24,256,256]{2,1,0:T(8,128)} fusion(f32[24,256,256]{2,1,0:T(8,128)} %fusion.4, f32[24,256,256]{2,1,0:T(8,128)} %bitcast.61, f32[24,2,256,256]{3,2,1,0:T(8,128)S(1)} %copy-done.2), kind=kOutput, calls=%fused_computation.18 | convolution fusion | flops 4833411072 | bytes 25165824 | tf_op jit(solution)/shard_map/fij,fjk->fik/dot_general | solution.py:15
  398.8 0.0 copy-start.4
  398.8 12.8 %fusion.2 = f32[24,256,256]{2,1,0:T(8,128)S(1)} fusion(f32[24,256,256]{2,1,0:T(8,128)} %fusion.4, f32[24,256,256]{2,1,0:T(8,128)} %fusion.10, f32[256,256]{1,0:T(8,128)S(1)} %fusion.14), kind=kOutput, calls=%fused_computation.10 | convolution fusion | flops 4833411072 | bytes 19136512 | tf_op jit(solution)/shard_map/fij,fjk->fik/dot_general | solution.py:16
  411.6 0.0 copy-done.4
  411.6 5.9 fusion.26
  417.5 0.0 copy-start.3
  417.5 4.2 fusion.6
  421.7 2.4 fusion.27
  424.2 0.0 copy-done.3
  424.2 0.1 reduce_sum.35
  424.3 0.0 copy-start.5
  424.3 3.2 copy.25
  427.5 2.9 gather_fusion.1
  430.4 0.0 copy-done.5
  430.4 0.1 copy.26
  430.5 0.1 reshape.293
  430.6 0.0 copy-start.1
  430.6 3.9 scatter_custom_fusion.1
  434.5 0.0 all-reduce.2.cloned.1.call-update
  434.5 0.0 all-gather.3.cloned.1.call-start
  434.6 154.5 %all-reduce.2.cloned.1.call-done = f32[24576]{0:T(1024)} async-done(((f32[24576]{0:T(1024)}), f32[24576]{0:T(1024)}) %all-reduce.2.cloned.1.call-update) | async-done | bytes 98320 | tf_op jit(solution)/shard_map/psum | solution.py:31
  589.1 3.6 gather_fusion.2
  592.7 0.1 reshape.299
  592.8 1.1 multiply_multiply_fusion
  593.8 0.8 reshape.300
  594.7 0.0 all-gather.3.cloned.1.call-update
  594.7 156.2 %all-gather.3.cloned.1.call-done = f32[32,4,9216]{2,1,0:T(4,128)} async-done(((f32[1,4,9216]{2,1,0:T(4,128)}), f32[32,4,9216]{2,1,0:T(4,128)}) %all-gather.3.cloned.1.call-update) | async-done | bytes 4718608 | tf_op jit(solution)/shard_map/all_gather | solution.py:72
  750.9 5.6 reshape.301
  756.5 0.0 copy-done.1
  (9 shorter events, 0.1 us)
Async XLA Ops:
  7.2 53.3 %copy-start = (f32[4,6,96,256]{3,2,1,0:T(8,128)S(1)}, f32[4,6,96,256]{3,2,1,0:T(8,128)}, u32[]{:S(2)}) copy-start(f32[4,6,96,256]{3,2,1,0:T(8,128)} %param.7) | copy-start | bytes 7077892
  50.9 9.3 %copy-start.6 = (s32[4,96]{1,0:T(4,128)S(1)}, s32[4,96]{1,0:T(4,128)}, u32[]{:S(2)}) copy-start(s32[4,96]{1,0:T(4,128)} %param.9) | copy-start | bytes 4612
  50.9 282.1 %all-to-all-start = ((f32[32,1,2,256,256]{4,3,2,1,0:T(8,128)}), f32[32,1,2,256,256]{4,3,2,1,0:T(8,128)}, u32[]{:S(2)}, u32[]{:S(2)}) async-start(f32[32,1,2,256,256]{4,3,2,1,0:T(8,128)} %bitcast.57), calls=%async_computation | async-start | bytes 33554432 | tf_op jit(solution)/shard_map/all_to_all | solution.py:58
  60.2 528.9 %all-reduce.2.cloned.1.call-start = ((), (), s32[]{:S(2)}) async-start(), calls=%async_computation.1 | async-start | bytes 196608 | tf_op jit(solution)/shard_map/psum | solution.py:31
  346.5 10.5 %copy-start.2 = (f32[24,2,256,256]{3,2,1,0:T(8,128)S(1)}, f32[24,2,256,256]{3,2,1,0:T(8,128)}, u32[]{:S(2)}) copy-start(f32[24,2,256,256]{3,2,1,0:T(8,128)} %gather_fusion) | copy-start | bytes 37748740
  398.8 12.8 %copy-start.4 = (f32[24,96,256]{2,1,0:T(8,128)S(1)}, f32[24,96,256]{2,1,0:T(8,128)}, u32[]{:S(2)}) copy-start(f32[24,96,256]{2,1,0:T(8,128)} %fusion.25) | copy-start | bytes 7077892
  417.5 6.7 copy-start.3
  424.3 6.1 copy-start.5
  430.6 325.9 %copy-start.1 = (f32[4,6,96,256]{3,2,1,0:T(8,128)S(1)}, f32[4,6,96,256]{3,2,1,0:T(8,128)}, u32[]{:S(2)}) copy-start(f32[4,6,96,256]{3,2,1,0:T(8,128)} %param.7) | copy-start | bytes 7077892
  434.5 316.3 %all-gather.3.cloned.1.call-start = ((), (), s32[]{:S(2)}) async-start(), calls=%async_computation.2 | async-start | bytes 4866048 | tf_op jit(solution)/shard_map/all_gather | solution.py:72
Sparse Core Ops, SparseCore 0:
  434.6 154.4 all-reduce.1
  594.8 155.9 all-gather.2
where the time goes:
time: 770 us; the launch traced here: 764 us
  waiting for transfers between devices  573 us (74%)
  matrix products  77.3 us (10%)
  local copies, waits for them, and re-layouts  62.8 us (8%)
  other arithmetic  26.5 us (3%)
  between operations  14.5 us (2%)
  starting transfers between devices  9.35 us (1%)
    all_to_all x1, waiting for transfers between devices, local(): lax.all_to_all(buffer, 'member', split_axis=0, concat_axis=0, tiled=True)  262 us
    all_gather x1, waiting for transfers between devices, local(): lax.all_gather(scaled.reshape(sub_count, prim_count * prim_count), 'membe...  156 us
    psum x1, waiting for transfers between devices, assemble_diagonal(): return lax.psum(local_diagonal, ('group', 'member'))  155 us
    dot_general x2, matrix products, inverse_sweeps(): jnp.einsum('fij,fjk->fik', summed, current, precision=FULL_PRECISION)  27.8 us
    dot_general x2, matrix products, inverse_sweeps(): jnp.einsum('fij,fjk->fik', current, doubled - applied, precision=FULL_PRE...  26.8 us
    scatter x1, local copies, waits for them, and re-layouts, local(): buffer = jnp.zeros((members, capacity) + stacked.shape[1:], jnp.float32)....  23.2 us
  transfers between devices with their start and end apart: 3, of which 3 were waited for; matrix products, arithmetic and copies ran while one was open for 1% of the time, Pallas kernels for 0%

commit v1 on v0

--- a/solution.py
+++ b/solution.py
@@ -28,7 +28,7 @@
 
 
 def assemble_diagonal(local_diagonal):
-    return lax.psum(local_diagonal, ("group", "member"))
+    return lax.psum(lax.psum(local_diagonal, "group"), "member")
 
 
 def local(face_schur, face_inverse, face_basis, partner, prim_index):

time: 770 us -> 950 us (1.23)
  waiting for transfers between devices: 573 us -> 753 us
    psum x1 -> x2, waiting for transfers between devices: 155 us -> 335 us  [assemble_diagonal(): return lax.psum(lax.psum(local_diagonal, 'group'), 'member')]
  transfers between devices with their start and end apart: 3 -> 4, of which waited for: 3 -> 4; matrix products, arithmetic and copies ran while one was open for 1% -> 1% of each run, Pallas kernels for 0% -> 0%
where the time goes in v1:
time: 950 us; the launch traced here: 944 us
  waiting for transfers between devices  753 us (79%)
  matrix products  77.3 us (8%)
  local copies, waits for them, and re-layouts  62.8 us (7%)
  other arithmetic  26.5 us (3%)
  between operations  14.2 us (1%)
    psum x2, waiting for transfers between devices, assemble_diagonal(): return lax.psum(lax.psum(local_diagonal, 'group'), 'member')  335 us
    all_to_all x1, waiting for transfers between devices, local(): lax.all_to_all(buffer, 'member', split_axis=0, concat_axis=0, tiled=True)  263 us
    all_gather x1, waiting for transfers between devices, local(): lax.all_gather(scaled.reshape(sub_count, prim_count * prim_count), 'membe...  156 us
    dot_general x2, matrix products, inverse_sweeps(): jnp.einsum('fij,fjk->fik', summed, current, precision=FULL_PRECISION)  27.8 us
    dot_general x2, matrix products, inverse_sweeps(): jnp.einsum('fij,fjk->fik', current, doubled - applied, precision=FULL_PRE...  26.8 us
    scatter x1, local copies, waits for them, and re-layouts, local(): buffer = jnp.zeros((members, capacity) + stacked.shape[1:], jnp.float32)....  23.2 us
  transfers between devices with their start and end apart: 4, of which 4 were waited for; matrix products, arithmetic and copies ran while one was open for 1% of the time, Pallas kernels for 0%

profile of v1, /device:TPU:0, one launch (start us, length us, event | category | flops | bytes accessed | tf_op | source)
XLA Modules:
  0.0 943.7 jit_solution(1446920627944395618)
XLA Ops:
  7.2 0.0 copy-start
  7.2 0.8 broadcast_divide_fusion
  8.0 0.7 compare_and_fusion.2
  8.7 0.1 div.30
  8.8 0.1 div.29
  8.9 0.1 rem.85
  9.0 0.1 ne.108
  9.1 0.1 and.74
  9.2 0.2 convert_reduce_fusion
  9.4 10.6 %pad_maximum_fusion = f32[24,2,256,256]{3,2,1,0:T(8,128)} fusion(f32[24,1,256,256]{3,2,1,0:T(8,128)} %bitcast.62, f32[24,1,256,256]{3,2,1,0:T(8,128)} %bitcast.58), kind=kLoop, calls=%fused_computation.5 | loop fusion | flops 3145728 | bytes 25165824 | tf_op jit(solution)/shard_map/stack | solution.py:52
  20.0 7.8 broadcast.301
  27.7 23.2 %scatter_fusion = f32[32,2,256,256]{3,2,1,0:T(8,128)} fusion(f32[32,2,256,256]{3,2,1,0:T(8,128)} %broadcast.301, s32[24]{0:T(128)S(1)} %fusion.24, f32[24,2,256,256]{3,2,1,0:T(8,128)} %pad_maximum_fusion), kind=kCustom, calls=%fused_computation.3 | custom fusion | bytes 37748832 | tf_op jit(solution)/shard_map/scatter | solution.py:56
  50.9 0.0 copy-start.6
  50.9 9.3 all-to-all-start
  60.2 0.0 all-reduce.3.cloned.1.call-start
  60.2 0.0 copy-done.6
  60.2 0.1 reshape.256
  60.4 0.0 copy-done
  60.4 10.1 %fusion.25 = f32[24,96,256]{2,1,0:T(8,128)} fusion(f32[24,96,256]{2,1,0:T(8,128)S(1)} %bitcast.56, f32[24,256,256]{2,1,0:T(8,128)} %bitcast.59), kind=kOutput, calls=%fused_computation.59 | convolution fusion | flops 1811939328 | bytes 11010048 | tf_op jit(solution)/shard_map/fck,fjk->fcj/dot_general | solution.py:23
  70.5 262.6 %all-to-all-done = f32[32,1,2,256,256]{4,3,2,1,0:T(8,128)} async-done(((f32[32,1,2,256,256]{4,3,2,1,0:T(8,128)}), f32[32,1,2,256,256]{4,3,2,1,0:T(8,128)}, u32[]{:S(2)}, u32[]{:S(2)}) %all-to-all-start) | async-done | bytes 16777248 | tf_op jit(solution)/shard_map/all_to_all | solution.py:58
  333.0 13.5 %gather_fusion = f32[24,2,256,256]{3,2,1,0:T(8,128)} fusion(f32[32,1,2,256,256]{4,3,2,1,0:T(8,128)} %all-to-all-done, s32[24]{0:T(128)S(1)} %get-tuple-element.4), kind=kCustom, calls=%fused_computation | custom fusion | bytes 25166016 | tf_op jit(solution)/shard_map/gather | solution.py:59
  346.5 0.0 copy-start.2
  346.5 9.0 fusion.1
  355.5 1.4 copy-done.2
  357.0 13.8 %fusion.12 = f32[24,256,256]{2,1,0:T(8,128)} fusion(f32[24,256,256]{2,1,0:T(8,128)} %fusion.1, f32[24,256,256]{2,1,0:T(8,128)} %bitcast.60, f32[24,2,256,256]{3,2,1,0:T(8,128)S(1)} %copy-done.2), kind=kOutput, calls=%fused_computation.19 | convolution fusion | flops 4833411072 | bytes 25165824 | tf_op jit(solution)/shard_map/fij,fjk->fik/dot_general | solution.py:15
  370.7 14.0 %fusion.4 = f32[24,256,256]{2,1,0:T(8,128)} fusion(f32[24,256,256]{2,1,0:T(8,128)} %fusion.1, f32[24,256,256]{2,1,0:T(8,128)} %fusion.12, f32[256,256]{1,0:T(8,128)S(1)} %fusion.14), kind=kOutput, calls=%fused_computation.12 | convolution fusion | flops 4833411072 | bytes 19136512 | tf_op jit(solution)/shard_map/fij,fjk->fik/dot_general | solution.py:16
  384.8 14.0 %fusion.10 = f32[24,256,256]{2,1,0:T(8,128)} fusion(f32[24,256,256]{2,1,0:T(8,128)} %fusion.4, f32[24,256,256]{2,1,0:T(8,128)} %bitcast.61, f32[24,2,256,256]{3,2,1,0:T(8,128)S(1)} %copy-done.2), kind=kOutput, calls=%fused_computation.18 | convolution fusion | flops 4833411072 | bytes 25165824 | tf_op jit(solution)/shard_map/fij,fjk->fik/dot_general | solution.py:15
  398.8 0.0 copy-start.4
  398.8 12.8 %fusion.2 = f32[24,256,256]{2,1,0:T(8,128)S(1)} fusion(f32[24,256,256]{2,1,0:T(8,128)} %fusion.4, f32[24,256,256]{2,1,0:T(8,128)} %fusion.10, f32[256,256]{1,0:T(8,128)S(1)} %fusion.14), kind=kOutput, calls=%fused_computation.10 | convolution fusion | flops 4833411072 | bytes 19136512 | tf_op jit(solution)/shard_map/fij,fjk->fik/dot_general | solution.py:16
  411.6 0.0 copy-done.4
  411.6 5.9 fusion.26
  417.5 0.0 copy-start.3
  417.5 4.2 fusion.6
  421.7 2.4 fusion.27
  424.2 0.0 copy-done.3
  424.2 0.1 reduce_sum.35
  424.3 0.0 copy-start.5
  424.3 3.2 copy.25
  427.5 2.9 gather_fusion.1
  430.4 0.0 copy-done.5
  430.4 0.1 copy.26
  430.5 0.1 reshape.293
  430.6 3.9 scatter_custom_fusion.1
  434.5 0.0 all-reduce.3.cloned.1.call-update
  434.5 0.0 copy-start.1
  434.5 0.0 all-reduce.5.cloned.1.call-start
  434.6 0.1 reshape.273
  434.7 55.2 %all-reduce.3.cloned.1.call-done = f32[24576]{0:T(1024)} async-done(((f32[24576]{0:T(1024)}), f32[24576]{0:T(1024)}) %all-reduce.3.cloned.1.call-update) | async-done | bytes 98320 | tf_op jit(solution)/shard_map/psum | solution.py:31
  489.9 0.0 all-reduce.5.cloned.1.call-update
  489.9 0.0 all-gather.3.cloned.1.call-start
  490.0 279.3 %all-reduce.5.cloned.1.call-done = f32[24576]{0:T(1024)} async-done(((f32[24576]{0:T(1024)}), f32[24576]{0:T(1024)}) %all-reduce.5.cloned.1.call-update) | async-done | bytes 98320 | tf_op jit(solution)/shard_map/psum | solution.py:31
  769.3 3.6 gather_fusion.2
  772.9 0.1 reshape.299
  773.0 1.1 multiply_multiply_fusion
  774.0 0.8 reshape.300
  774.9 0.0 all-gather.3.cloned.1.call-update
  774.9 156.3 %all-gather.3.cloned.1.call-done = f32[32,4,9216]{2,1,0:T(4,128)} async-done(((f32[1,4,9216]{2,1,0:T(4,128)}), f32[32,4,9216]{2,1,0:T(4,128)}) %all-gather.3.cloned.1.call-update) | async-done | bytes 4718608 | tf_op jit(solution)/shard_map/all_gather | solution.py:72
  931.2 5.6 reshape.301
  936.9 0.0 copy-done.1
  (9 shorter events, 0.1 us)
Async XLA Ops:
  7.2 53.2 %copy-start = (f32[4,6,96,256]{3,2,1,0:T(8,128)S(1)}, f32[4,6,96,256]{3,2,1,0:T(8,128)}, u32[]{:S(2)}) copy-start(f32[4,6,96,256]{3,2,1,0:T(8,128)} %param.7) | copy-start | bytes 7077892
  50.9 9.3 copy-start.6
  50.9 282.1 %all-to-all-start = ((f32[32,1,2,256,256]{4,3,2,1,0:T(8,128)}), f32[32,1,2,256,256]{4,3,2,1,0:T(8,128)}, u32[]{:S(2)}, u32[]{:S(2)}) async-start(f32[32,1,2,256,256]{4,3,2,1,0:T(8,128)} %bitcast.57), calls=%async_computation | async-start | bytes 33554432 | tf_op jit(solution)/shard_map/all_to_all | solution.py:58
  60.2 429.7 %all-reduce.3.cloned.1.call-start = ((), (), s32[]{:S(2)}) async-start(), calls=%async_computation.1 | async-start | bytes 196608 | tf_op jit(solution)/shard_map/psum | solution.py:31
  346.5 10.5 %copy-start.2 = (f32[24,2,256,256]{3,2,1,0:T(8,128)S(1)}, f32[24,2,256,256]{3,2,1,0:T(8,128)}, u32[]{:S(2)}) copy-start(f32[24,2,256,256]{3,2,1,0:T(8,128)} %gather_fusion) | copy-start | bytes 37748740
  398.8 12.8 %copy-start.4 = (f32[24,96,256]{2,1,0:T(8,128)S(1)}, f32[24,96,256]{2,1,0:T(8,128)}, u32[]{:S(2)}) copy-start(f32[24,96,256]{2,1,0:T(8,128)} %fusion.25) | copy-start | bytes 7077892
  417.5 6.7 copy-start.3
  424.3 6.1 copy-start.5
  434.5 502.4 %copy-start.1 = (f32[4,6,96,256]{3,2,1,0:T(8,128)S(1)}, f32[4,6,96,256]{3,2,1,0:T(8,128)}, u32[]{:S(2)}) copy-start(f32[4,6,96,256]{3,2,1,0:T(8,128)} %param.7) | copy-start | bytes 7077892
  434.5 334.8 %all-reduce.5.cloned.1.call-start = ((), (), s32[]{:S(2)}) async-start(), calls=%async_computation.2 | async-start | bytes 196608 | tf_op jit(solution)/shard_map/psum | solution.py:31
  489.9 441.3 %all-gather.3.cloned.1.call-start = ((), (), s32[]{:S(2)}) async-start(), calls=%async_computation.3 | async-start | bytes 4866048 | tf_op jit(solution)/shard_map/all_gather | solution.py:72
Sparse Core Ops, SparseCore 0:
  434.6 55.2 all-reduce.2
  492.4 276.9 all-reduce.4
  775.0 156.1 all-gather.2
